TPU v7x, 512 devices: a whole 4x4x16 slice. The times are simulated.
512 devices in a mesh: chord: 64 (over z, x), span: 8 (over y, core).
Axes of the slice: x: 4, y: 4, z: 16, core: 2. Of those that a mesh axis runs over, the one named last changes fastest.
Arguments:
- adjoint_init: bfloat16 [64, 8, 3, 625, 128], P('chord', 'span'), may hold values from -6 to 6
- adjoint_rhs: bfloat16 [64, 8, 3, 625, 128], P('chord', 'span'), may hold values from -6 to 6
- block_inverse: bfloat16 [64, 8, 3, 625, 625], P('chord', 'span'), as said below
- flux_jacobian: float32 [64, 8, 3, 6, 5, 5, 25], P('chord', 'span'), may hold values from -2.5 to 2.5
- trace_ops: bfloat16 [4, 6, 25, 125], replicated, may hold values from -0.5 to 0.5
- shape_jacobian: bfloat16 [64, 8, 3, 81, 625], P('chord', 'span'), may hold values from -0.25 to 0.25
- element_order: int32 [64, 8, 3], P('chord', 'span'), may hold values from 1 to 4, as said below
- face_adjacency: int32 [64, 8, 3, 6], P('chord', 'span'), may hold values from -1 to 2, as said below
- node_owner: int32 [64, 8, 3, 27], P('chord', 'span'), may hold values from 0 to 159, as said below
Outputs:
- smoothed_adjoint: bfloat16 [64, 8, 3, 625, 128], P('chord', 'span')
- node_sensitivity: float32 [64, 8, 32, 3, 128], P('chord', 'span')
Inputs may be any that keep to these rules, and one draw needn't show every extreme that they name: `element_order`: live unknowns of an element are its first 5 * min(125, (order + 1)**3). `face_adjacency`: entry [e, f] names the element beside face f in the partition that f faces (faces 0 and 1 previous and next along chord, cyclic; 2 and 3 previous and next along span; 4 and 5 the same partition), which meets it with its face f xor 1; -1 marks a boundary face (span ends, wall, far field). `node_owner`: entry k * 32 + i: owned node i of partition k, k = 0 the element's own, 1 and 2 previous and next along chord, 3 and 4 previous and next along span; k is never 3 on the first span partition nor 4 on the last. `block_inverse`: only the rows and columns of live unknowns act.
All inputs are finite; a program needn't handle non-finite values.
Results may differ from a plain program's by a relative error of at most 0.0069.
Values may be sent and summed in bfloat16 or wider, within the bound.
No kernel may reach another device: no remote copies, remote signals or barrier semaphores. Data moves between devices by JAX's collectives and lax.ppermute only.
A program may use at most 64 MiB of HBM per device.

v0:
```python
import jax
import jax.numpy as jnp
from jax import lax
from jax.experimental import pallas as pl
from jax.experimental.pallas import tpu as pltpu
from jax.sharding import PartitionSpec as P


ELEMS = 3
NODES = 125
VARS = 5
BLOCK = 625
PTS = 25
GEO = 27
OWNED = 32
RHS = 128
FROWS = 128
SENS = 3 * OWNED
PITCH = 32

ISSUE_ORDER = ("B", "A", "D", "C")
SLOT_AXIS = {"A": "chord", "B": "chord", "C": "span", "D": "span"}
F32 = jnp.float32
BF16 = jnp.bfloat16


def swap_pairs(slot, size):
    cyclic = SLOT_AXIS[slot] == "chord"
    first = 0 if slot in "AC" else 1
    last = size if cyclic else size - 1
    pairs = []
    for i in range(first, last, 2):
        j = (i + 1) % size
        pairs += [(i, j), (j, i)]
    return pairs


def exchange(sends):
    received = []
    for i, slot in enumerate(ISSUE_ORDER):
        axis = SLOT_AXIS[slot]
        received.append(lax.ppermute(sends[i], axis, swap_pairs(slot, lax.axis_size(axis))))
    return received


def slot_faces():
    chord_odd = lax.axis_index("chord") % 2
    span_odd = lax.axis_index("span") % 2
    faces = {"A": 1 - chord_odd, "B": chord_odd, "C": 3 - span_odd, "D": 2 + span_odd}
    return [faces[slot] for slot in ISSUE_ORDER]


def dot(a, b, dims=((1,), (0,))):
    return lax.dot_general(a, b, (dims, ((), ())), preferred_element_type=F32)


def iota(shape, dim):
    return lax.broadcasted_iota(jnp.int32, shape, dim)


def one_of(value, choices):
    hit = value == choices[0]
    for choice in choices[1:]:
        hit = hit | (value == choice)
    return hit


def point_spread(order):
    gap = 4 * iota((FROWS, PTS * 4), 0) + order - 1 - iota((FROWS, PTS * 4), 1)
    return one_of(gap, [v * PTS * 4 for v in range(VARS)]).astype(BF16)


def node_spread(shape, node_dim):
    gap = iota(shape, 1 - node_dim) - VARS * iota(shape, node_dim)
    return ((gap >= 0) & (gap < VARS)).astype(BF16)


def live_mask(order, shape):
    count = VARS * jnp.minimum((order + 1) * (order + 1) * (order + 1), NODES)
    return iota(shape, 0) < count


def variable_of(unknown):
    node = ((unknown.astype(F32) + 0.5) * (1.0 / VARS)).astype(jnp.int32)
    return unknown - VARS * node


def build_trace_rows(rows_ref, order_ref, faces, trace_ref):
    count = len(faces)
    spreads = [point_spread(order_ref[0, 0, e]) for e in range(ELEMS)]
    for s, face in enumerate(faces):
        levels = trace_ref[face].astype(F32).reshape(PTS * 4, NODES).astype(BF16)
        for e in range(ELEMS):
            at = (e * count + s) * FROWS
            rows_ref[at : at + FROWS, :] = dot(spreads[e], levels).astype(BF16)


def build_face_operator(op_ref, faces, flux_ref, rows_ref, line_ref):
    count = len(faces)
    line_ref[...] = jnp.zeros(line_ref.shape, F32)
    for e in range(ELEMS):
        for s, face in enumerate(faces):
            for w in range(VARS):
                first = ((e * 6 + face) * VARS + w) * VARS
                line_ref[e * count + s, w, 0:VARS, 0:PTS] = flux_ref[pl.ds(first, VARS), 0, :]
    columns = []
    for w in range(VARS):
        lines = []
        for i in range(ELEMS * count):
            moved = pltpu.roll(line_ref[i, w], 0, 1, stride=PTS // 2, stride_axis=0)
            moved = pltpu.roll(moved, 0, 1, stride=PTS - PTS // 2, stride_axis=0)
            lines.append(jnp.sum(moved, axis=0, keepdims=True))
        columns.append(jnp.concatenate(lines, axis=1))
    flux_lines = jnp.concatenate(columns, axis=0)
    high = flux_lines.astype(BF16)
    low = (flux_lines - high.astype(F32)).astype(BF16)
    pair = jnp.concatenate([high.astype(F32), low.astype(F32)], axis=0)
    line = iota((2 * VARS, BLOCK), 0)
    picks = (variable_of(iota((2 * VARS, BLOCK), 1)) == variable_of(line)).astype(BF16)
    factors = dot(pair.T.astype(BF16), picks)
    nodes = node_spread((NODES, BLOCK), 0)
    wide = dot(rows_ref[...], nodes)
    op = (wide * factors).astype(BF16)
    for e in range(ELEMS):
        op_ref[e] = op[e * count * FROWS : (e + 1) * count * FROWS]


def build_trace_points(points_ref, order_ref, faces, trace_ref):
    for s, face in enumerate(faces):
        levels = trace_ref[face].astype(F32).reshape(PTS * 4, NODES).astype(BF16)
        for e in range(ELEMS):
            shape = (PITCH, PTS * 4)
            pick = 4 * iota(shape, 0) + order_ref[0, 0, e] - 1 == iota(shape, 1)
            rows = dot(pick.astype(F32).astype(BF16), levels).astype(BF16)
            points_ref[e, s * PITCH : (s + 1) * PITCH, :] = rows


def coupling(points, inflows, wide_ref, out_ref):
    for s, inflow in enumerate(inflows):
        rows = inflow.astype(F32)
        for v in range(VARS):
            at = slice(s * PITCH, s * PITCH + PTS)
            wide_ref[at, v * RHS : (v + 1) * RHS] = rows[v * PTS : (v + 1) * PTS]
    sums = dot(points, wide_ref[...].astype(BF16), ((0,), (0,)))
    for v in range(VARS):
        out_ref[pl.ds(v, NODES, stride=VARS), :] = sums[:, v * RHS : (v + 1) * RHS]
    return out_ref[...]


def start_copies(pairs, sems):
    copies = [pltpu.make_async_copy(src, dst, sems.at[i]) for i, (src, dst) in enumerate(pairs)]
    for copy in copies:
        copy.start()
    return copies


def first_tiles_kernel(order_hbm, adjoint_hbm, flux_hbm, trace_hbm, *refs):
    sends, (op_ref, adjoint_ref, flux_ref, trace_ref) = refs[:4], refs[4:8]
    rows_ref, line_ref, order_ref, sems = refs[8:]
    sources = (order_hbm, trace_hbm, flux_hbm, adjoint_hbm)
    copies = start_copies(zip(sources, (order_ref, trace_ref, flux_ref, adjoint_ref)), sems)
    faces = slot_faces()
    copies[0].wait()
    copies[1].wait()
    build_trace_rows(rows_ref, order_ref, faces, trace_ref)
    copies[2].wait()
    build_face_operator(op_ref, faces, flux_ref, rows_ref, line_ref)
    copies[3].wait()
    for e in range(ELEMS):
        live = live_mask(order_ref[0, 0, e], (BLOCK, RHS))
        adjoint = jnp.where(live, adjoint_ref[0, 0, e], jnp.zeros((), BF16))
        tiles = dot(op_ref[e], adjoint).astype(BF16)
        for s in range(4):
            sends[s][e] = tiles[s * FROWS : (s + 1) * FROWS]


def local_driven(near_ref, adjoints, rhs_ref, op_ref, points_ref, tile_ref, wide_ref, sum_ref, out_ref):
    wide_ref[...] = jnp.zeros(wide_ref.shape, F32)
    for e in range(ELEMS):
        tile_ref[e] = dot(op_ref[e], adjoints(e)).astype(BF16)
    for e in range(ELEMS):
        pieces = []
        for face in (4, 5):
            near = near_ref[e, 0, face]
            at = (5 - face) * FROWS
            picked = tile_ref[jnp.maximum(near, 0), at : at + FROWS, :]
            pieces.append(jnp.where(near >= 0, picked, jnp.zeros((), BF16)))
        total = coupling(points_ref[e], pieces, wide_ref.at[e], sum_ref.at[e])
        out_ref[e] = rhs_ref[0, 0, e].astype(F32) - total


def prepare_kernel(order_hbm, near_hbm, rhs_hbm, inverse_hbm, adjoint_ref, flux_ref, trace_ref, *refs):
    base_ref, points_ref, local_op_ref, local_points_ref, rhs_ref, inverse_ref = refs[:6]
    rows_ref, line_ref, tile_ref, wide_ref, sum_ref, order_ref, near_ref, sems = refs[6:]
    sources = (order_hbm, near_hbm, rhs_hbm, inverse_hbm)
    copies = start_copies(zip(sources, (order_ref, near_ref, rhs_ref, inverse_ref)), sems)
    copies[0].wait()
    build_trace_rows(rows_ref, order_ref, [4, 5], trace_ref)
    build_face_operator(local_op_ref, [4, 5], flux_ref, rows_ref, line_ref)
    build_trace_points(local_points_ref, order_ref, [4, 5], trace_ref)
    build_trace_points(points_ref, order_ref, slot_faces(), trace_ref)

    def adjoints(e):
        live = live_mask(order_ref[0, 0, e], (BLOCK, RHS))
        return jnp.where(live, adjoint_ref[0, 0, e], jnp.zeros((), BF16))

    copies[1].wait()
    copies[2].wait()
    local_driven(
        near_ref, adjoints, rhs_ref, local_op_ref, local_points_ref,
        tile_ref, wide_ref, sum_ref, base_ref,
    )
    copies[3].wait()


def local_kernel(
    order_ref, near_ref, adjoint_ref, rhs_ref, local_op_ref, local_points_ref,
    base_ref, tile_ref, wide_ref, sum_ref,
):
    local_driven(
        near_ref, lambda e: adjoint_ref[e], rhs_ref, local_op_ref, local_points_ref,
        tile_ref, wide_ref, sum_ref, base_ref,
    )


def solve_blocks(
    faces, order_ref, near_ref, base_ref, arrived, points_ref, inverse_ref, wide_ref, sum_ref
):
    wide_ref[...] = jnp.zeros(wide_ref.shape, F32)
    driven = []
    for e in range(ELEMS):
        pieces = []
        for s, face in enumerate(faces):
            near = near_ref[e, 0, face]
            picked = arrived[s][jnp.maximum(near, 0)]
            pieces.append(jnp.where(near >= 0, picked, jnp.zeros((), BF16)))
        total = coupling(points_ref[e], pieces, wide_ref.at[e], sum_ref.at[e])
        live = live_mask(order_ref[0, 0, e], (BLOCK, RHS))
        driven.append(jnp.where(live, base_ref[e] - total, 0.0).astype(BF16))
    solved = []
    for e in range(ELEMS):
        live = live_mask(order_ref[0, 0, e], (BLOCK, RHS))
        solved.append(jnp.where(live, dot(inverse_ref[0, 0, e], driven[e]), 0.0).astype(BF16))
    return solved


def sweep_kernel(order_ref, near_ref, base_ref, a0, a1, a2, a3, points_ref, inverse_ref, op_ref, *refs):
    sends, (adjoint_ref, wide_ref, sum_ref) = refs[:4], refs[4:]
    solved = solve_blocks(
        slot_faces(), order_ref, near_ref, base_ref, (a0, a1, a2, a3), points_ref, inverse_ref,
        wide_ref, sum_ref,
    )
    for e in range(ELEMS):
        adjoint_ref[e] = solved[e]
        tiles = dot(op_ref[e], solved[e]).astype(BF16)
        for s in range(4):
            sends[s][e] = tiles[s * FROWS : (s + 1) * FROWS]


def last_kernel(
    order_ref, near_ref, base_ref, a0, a1, a2, a3, points_ref, inverse_ref, shape_ref, owner_ref, *refs
):
    adjoint_ref, own_ref, sends, (wide_ref, sum_ref) = refs[0], refs[1], refs[2:6], refs[6:]
    faces = slot_faces()
    owner = owner_ref[:, 0, :].astype(F32).astype(BF16)
    gap = iota((GEO, 3 * GEO), 1) - 3 * iota((GEO, 3 * GEO), 0)
    owners = dot(owner, ((gap >= 0) & (gap < 3)).astype(BF16))
    row = iota((SENS, 3 * GEO), 0)
    coordinate = (row >= OWNED).astype(jnp.int32) + (row >= 2 * OWNED).astype(jnp.int32)
    slot = (row - OWNED * coordinate).astype(F32)
    column = iota((SENS, 3 * GEO), 1)
    fits = column - 3 * ((column.astype(F32) + 0.5) * (1.0 / 3)).astype(jnp.int32) == coordinate
    solved = solve_blocks(
        faces, order_ref, near_ref, base_ref, (a0, a1, a2, a3), points_ref, inverse_ref,
        wide_ref, sum_ref,
    )
    total = jnp.zeros((5 * SENS, RHS), F32)
    for e in range(ELEMS):
        adjoint_ref[0, 0, e] = solved[e]
        partial = dot(shape_ref[0, 0, e], solved[e])
        high = partial.astype(BF16)
        low = (partial - high.astype(F32)).astype(BF16)
        picks = []
        for first in [0] + [OWNED * (face + 1) for face in faces]:
            hit = owners[e : e + 1, :] - jnp.asarray(first, jnp.int32).astype(F32) == slot
            picks.append((hit & fits).astype(F32).astype(BF16))
        picks = jnp.concatenate(picks, axis=0)
        total = total + dot(picks, high) + dot(picks, low)
    own_ref[...] = total[:SENS]
    for s in range(4):
        sends[s][...] = total[(s + 1) * SENS : (s + 2) * SENS].astype(BF16)


def sum_kernel(own_ref, a0, a1, a2, a3, out_ref):
    total = own_ref[...]
    for arrived in (a0, a1, a2, a3):
        total = total + arrived[...].astype(F32)
    for c in range(3):
        out_ref[0, 0, c] = total[c * OWNED : (c + 1) * OWNED]


SMEM = pl.BlockSpec(memory_space=pltpu.SMEM)
VMEM = pl.BlockSpec(memory_space=pltpu.VMEM)
ANY = pl.BlockSpec(memory_space=pl.ANY)
LIMIT = 24 * 1024 * 1024


def call(kernel, scalars, stored, held, outs, scratch=()):
    stored = [pltpu.with_memory_space_constraint(x, pltpu.HBM) for x in stored]
    held = [pltpu.with_memory_space_constraint(x, pltpu.VMEM) for x in held]
    return pl.pallas_call(
        kernel,
        in_specs=[SMEM] * len(scalars) + [ANY] * len(stored) + [VMEM] * len(held),
        out_specs=[VMEM] * len(outs),
        out_shape=outs,
        scratch_shapes=list(scratch),
        compiler_params=pltpu.CompilerParams(vmem_limit_bytes=LIMIT),
    )(*scalars, *stored, *held)


def body(
    adjoint_init,
    adjoint_rhs,
    block_inverse,
    flux_jacobian,
    trace_ops,
    shape_jacobian,
    element_order,
    face_adjacency,
    node_owner,
):
    held = pltpu.VMEM
    near = face_adjacency.reshape(ELEMS, 1, 6)
    owner = node_owner.reshape(ELEMS, 1, GEO)
    flux = flux_jacobian.reshape(ELEMS * 6 * VARS * VARS, 1, PTS)
    trace = jnp.transpose(trace_ops, (1, 2, 0, 3))
    face_send = [held((ELEMS, FROWS, RHS), BF16)] * 4
    base_shape = held((ELEMS, BLOCK, RHS), F32)
    near_sums = [pltpu.VMEM((ELEMS, 2 * PITCH, VARS * RHS), F32), pltpu.VMEM((ELEMS, BLOCK, RHS), F32)]
    far_sums = [pltpu.VMEM((ELEMS, 4 * PITCH, VARS * RHS), F32), pltpu.VMEM((ELEMS, BLOCK, RHS), F32)]
    order_smem = pltpu.SMEM(element_order.shape, jnp.int32)
    near_smem = pltpu.SMEM(near.shape, jnp.int32)
    *sends, face_op, adjoint, flux, trace = call(
        first_tiles_kernel,
        [],
        [element_order, adjoint_init, flux, trace],
        [],
        face_send
        + [
            held((ELEMS, 4 * FROWS, BLOCK), BF16),
            held(adjoint_init.shape, BF16),
            held(flux.shape, F32),
            held(trace.shape, BF16),
        ],
        [
            pltpu.VMEM((ELEMS * 4 * FROWS, NODES), BF16),
            pltpu.VMEM((ELEMS * 4, VARS, 8, 128), F32),
            order_smem,
            pltpu.SemaphoreType.DMA((4,)),
        ],
    )
    arrived = exchange(sends)
    base, points, local_op, local_points, rhs, inverse = call(
        prepare_kernel,
        [],
        [element_order, near, adjoint_rhs, block_inverse],
        [adjoint, flux, trace],
        [
            base_shape,
            held((ELEMS, 4 * PITCH, NODES), BF16),
            held((ELEMS, 2 * FROWS, BLOCK), BF16),
            held((ELEMS, 2 * PITCH, NODES), BF16),
            held(adjoint_rhs.shape, BF16),
            held(block_inverse.shape, BF16),
        ],
        [
            pltpu.VMEM((ELEMS * 2 * FROWS, NODES), BF16),
            pltpu.VMEM((ELEMS * 2, VARS, 8, 128), F32),
            pltpu.VMEM((ELEMS, 2 * FROWS, RHS), BF16),
            *near_sums,
            order_smem,
            near_smem,
            pltpu.SemaphoreType.DMA((4,)),
        ],
    )
    *sends, adjoint = call(
        sweep_kernel,
        [element_order, near],
        [],
        [base, *arrived, points, inverse, face_op],
        face_send + [held((ELEMS, BLOCK, RHS), BF16)],
        far_sums,
    )
    arrived = exchange(sends)
    (base,) = call(
        local_kernel,
        [element_order, near],
        [],
        [adjoint, rhs, local_op, local_points],
        [base_shape],
        [pltpu.VMEM((ELEMS, 2 * FROWS, RHS), BF16), *near_sums],
    )
    smoothed, own, *sends = call(
        last_kernel,
        [element_order, near],
        [],
        [base, *arrived, points, inverse, shape_jacobian, owner],
        [held((1, 1, ELEMS, BLOCK, RHS), BF16), held((SENS, RHS), F32)]
        + [held((SENS, RHS), BF16)] * 4,
        far_sums,
    )
    arrived = exchange(sends)
    (summed,) = call(
        sum_kernel, [], [], [own, *arrived], [jax.ShapeDtypeStruct((1, 1, 3, OWNED, RHS), F32)]
    )
    return smoothed, jnp.transpose(summed, (0, 1, 3, 2, 4))


def solution(mesh):
    placed = (
        P("chord", "span", None, None, None),
        P("chord", "span", None, None, None),
        P("chord", "span", None, None, None),
        P("chord", "span", None, None, None, None, None),
        P(),
        P("chord", "span", None, None, None),
        P("chord", "span", None),
        P("chord", "span", None, None),
        P("chord", "span", None, None),
    )
    return jax.shard_map(
        body,
        mesh=mesh,
        in_specs=placed,
        out_specs=(P("chord", "span", None, None, None), P("chord", "span", None, None, None)),
        check_vma=False,
    )
```

profile of v0, /device:TPU:1, one launch (start us, length us, event | category | flops | bytes accessed | tf_op | source)
XLA Modules:
  0.0 61.3 jit_solution(10536559509186798714)
XLA Ops:
  0.6 0.0 copy-start.2
  0.6 0.0 copy-start.1
  0.7 4.1 %shard_map.104 = (bf16[3,128,128]{2,1,0:T(8,128)(2,1)S(1)}, bf16[3,128,128]{2,1,0:T(8,128)(2,1)S(1)}, bf16[3,128,128]{2,1,0:T(8,128)(2,1)S(1)}, bf16[3,128,128]{...) custom-call(s32[1,1,3]{2,1,0:T(1,128)} %order_ref.5, ...), custom_call_target="tpu_custom_call" | custom-call | tf_op jit(solution)/shard_map/pallas_call | solution.py:311
  4.8 14.1 %collective-permute-start = (bf16[3,128,128]{2,1,0:T(8,128)(2,1)S(1)}, bf16[3,128,128]{2,1,0:T(8,128)(2,1)S(1)}, u32[]{:S(2)}, u32[]{:S(2)}) collective-permute-start(bf16[3,128,128]{2,1,0:T(8,128)(2,1)S(1)} %get-tuple-element.31), channel_id=1, source_target_pairs={{8,16},{16,8},{24,32},{32,24},{40,48},{48,40},{56,64},{64,56},{72,... | collective-permute-start | bytes 294920 | tf_op jit(solution)/shard_map/ppermute | solution.py:42
  18.9 1.9 %collective-permute-start.1 = (bf16[3,128,128]{2,1,0:T(8,128)(2,1)S(1)}, bf16[3,128,128]{2,1,0:T(8,128)(2,1)S(1)}, u32[]{:S(2)}, u32[]{:S(2)}) collective-permute-start(bf16[3,128,128]{2,1,0:T(8,128)(2,1)S(1)} %get-tuple-element.32), channel_id=1, source_target_pairs={{0,8},{8,0},{16,24},{24,16},{32,40},{40,32},{48,56},{56,48},{64,72... | collective-permute-start | bytes 294920 | tf_op jit(solution)/shard_map/ppermute | solution.py:42
  20.8 4.0 %collective-permute-start.2 = (bf16[3,128,128]{2,1,0:T(8,128)(2,1)S(1)}, bf16[3,128,128]{2,1,0:T(8,128)(2,1)S(1)}, u32[]{:S(2)}, u32[]{:S(2)}) collective-permute-start(bf16[3,128,128]{2,1,0:T(8,128)(2,1)S(1)} %get-tuple-element.33), channel_id=1, source_target_pairs={{1,2},{2,1},{3,4},{4,3},{5,6},{6,5},{9,10},{10,9},{11,12},{12,11},... | collective-permute-start | bytes 294920 | tf_op jit(solution)/shard_map/ppermute | solution.py:42
  24.9 1.9 %collective-permute-start.3 = (bf16[3,128,128]{2,1,0:T(8,128)(2,1)S(1)}, bf16[3,128,128]{2,1,0:T(8,128)(2,1)S(1)}, u32[]{:S(2)}, u32[]{:S(2)}) collective-permute-start(bf16[3,128,128]{2,1,0:T(8,128)(2,1)S(1)} %get-tuple-element.34), channel_id=1, source_target_pairs={{0,1},{1,0},{2,3},{3,2},{4,5},{5,4},{6,7},{7,6},{8,9},{9,8},{10,11... | collective-permute-start | bytes 294920 | tf_op jit(solution)/shard_map/ppermute | solution.py:42
  26.8 2.7 %shard_map.105 = (f32[3,625,128]{2,1,0:T(8,128)S(1)}, bf16[3,128,125]{2,1,0:T(8,128)(2,1)S(1)}, bf16[3,256,625]{2,1,0:T(8,128)(2,1)S(1)}, bf16[3,64,125]{2,1,0:T...) custom-call(s32[1,1,3]{2,1,0:T(1,128)} %order_ref.5, ...), custom_call_target="tpu_custom_call" | custom-call | tf_op jit(solution)/shard_map/pallas_call | solution.py:311
  29.5 0.0 collective-permute-done.a0
  29.6 0.0 collective-permute-done.1.a1
  29.6 0.0 collective-permute-done.3.a3
  29.6 2.3 %shard_map.106 = (bf16[3,128,128]{2,1,0:T(8,128)(2,1)S(1)}, bf16[3,128,128]{2,1,0:T(8,128)(2,1)S(1)}, bf16[3,128,128]{2,1,0:T(8,128)(2,1)S(1)}, bf16[3,128,128]{2,1,0:T(8,128)(2,1)S(1)}, bf16[3,625,128]{2,1,0:T(8,128)(2,1)S(1)}) custom-call(s32[1,1,3]{2,1,0:T(1,128)S(1)} %copy-done.2, s32[3,1,6]{2,1,0:T(1,128)S(1)} %bitcast.6, ...), custom_call_target="tpu_custom_call" | custom-call | tf_op jit(solution)/shard_map/pallas_call | solution.py:311
  31.9 0.0 copy-start
  31.9 0.0 copy-start.3
  31.9 3.1 %collective-permute-start.4 = (bf16[3,128,128]{2,1,0:T(8,128)(2,1)S(1)}, bf16[3,128,128]{2,1,0:T(8,128)(2,1)S(1)}, u32[]{:S(2)}, u32[]{:S(2)}) collective-permute-start(bf16[3,128,128]{2,1,0:T(8,128)(2,1)S(1)} %get-tuple-element.42), channel_id=1, source_target_pairs={{8,16},{16,8},{24,32},{32,24},{40,48},{48,40},{56,64},{64,56},{72,... | collective-permute-start | bytes 294920 | tf_op jit(solution)/shard_map/ppermute | solution.py:42
  35.0 2.6 %collective-permute-start.5 = (bf16[3,128,128]{2,1,0:T(8,128)(2,1)S(1)}, bf16[3,128,128]{2,1,0:T(8,128)(2,1)S(1)}, u32[]{:S(2)}, u32[]{:S(2)}) collective-permute-start(bf16[3,128,128]{2,1,0:T(8,128)(2,1)S(1)} %get-tuple-element.43), channel_id=1, source_target_pairs={{0,8},{8,0},{16,24},{24,16},{32,40},{40,32},{48,56},{56,48},{64,72... | collective-permute-start | bytes 294920 | tf_op jit(solution)/shard_map/ppermute | solution.py:42
  37.6 3.9 %collective-permute-start.6 = (bf16[3,128,128]{2,1,0:T(8,128)(2,1)S(1)}, bf16[3,128,128]{2,1,0:T(8,128)(2,1)S(1)}, u32[]{:S(2)}, u32[]{:S(2)}) collective-permute-start(bf16[3,128,128]{2,1,0:T(8,128)(2,1)S(1)} %get-tuple-element.44), channel_id=1, source_target_pairs={{1,2},{2,1},{3,4},{4,3},{5,6},{6,5},{9,10},{10,9},{11,12},{12,11},... | collective-permute-start | bytes 294920 | tf_op jit(solution)/shard_map/ppermute | solution.py:42
  41.5 1.9 %collective-permute-start.7 = (bf16[3,128,128]{2,1,0:T(8,128)(2,1)S(1)}, bf16[3,128,128]{2,1,0:T(8,128)(2,1)S(1)}, u32[]{:S(2)}, u32[]{:S(2)}) collective-permute-start(bf16[3,128,128]{2,1,0:T(8,128)(2,1)S(1)} %get-tuple-element.45), channel_id=1, source_target_pairs={{0,1},{1,0},{2,3},{3,2},{4,5},{5,4},{6,7},{7,6},{8,9},{9,8},{10,11... | collective-permute-start | bytes 294920 | tf_op jit(solution)/shard_map/ppermute | solution.py:42
  43.4 1.3 %shard_map.107.base_ref = f32[3,625,128]{2,1,0:T(8,128)S(1)} custom-call(s32[1,1,3]{2,1,0:T(1,128)S(1)} %copy-done.2, s32[3,1,6]{2,1,0:T(1,128)S(1)} %bitcast.7, bf16[3,625,128]{2,1,0:T(8,128)(2,1)S(1)} %get-tuple-element.38.adjoint_ref, bf16[1,1,3,625,128]{4,3,2,1,0:T(8,128)(2,1)S(1)} %get-tuple-element.39.rhs_ref, ...), custom_call_target="tpu_custom_call" | custom-call | tf_op jit(solution)/shard_map/pallas_call | solution.py:311
  44.7 0.0 collective-permute-done.4.a0
  44.7 0.0 collective-permute-done.5.a1
  44.8 0.0 collective-permute-done.7.a3
  44.8 2.3 %shard_map.108 = (bf16[1,1,3,625,128]{4,3,2,1,0:T(8,128)(2,1)S(1)}, f32[96,128]{1,0:T(8,128)S(1)}, bf16[96,128]{1,0:T(8,128)(2,1)S(1)}, bf16[96,128]{1,0:T(8,128...) custom-call(s32[1,1,3]{2,1,0:T(1,128)S(1)} %copy-done.2, s32[3,1,6]{2,1,0:T(1,128)S(1)} %bitcast.8, ...), custom_call_target="tpu_custom_call" | custom-call | tf_op jit(solution)/shard_map/pallas_call | solution.py:311
  47.1 5.0 %collective-permute-start.8 = (bf16[96,128]{1,0:T(8,128)(2,1)S(1)}, bf16[96,128]{1,0:T(8,128)(2,1)S(1)}, u32[]{:S(2)}, u32[]{:S(2)}) collective-permute-start(bf16[96,128]{1,0:T(8,128)(2,1)S(1)} %get-tuple-element.48), channel_id=1, source_target_pairs={{8,16},{16,8},{24,32},{32,24},{40,48},{48,40},{56,64},{64,56},{72,... | collective-permute-start | bytes 73736 | tf_op jit(solution)/shard_map/ppermute | solution.py:42
  52.1 1.9 %collective-permute-start.9 = (bf16[96,128]{1,0:T(8,128)(2,1)S(1)}, bf16[96,128]{1,0:T(8,128)(2,1)S(1)}, u32[]{:S(2)}, u32[]{:S(2)}) collective-permute-start(bf16[96,128]{1,0:T(8,128)(2,1)S(1)} %get-tuple-element.49), channel_id=1, source_target_pairs={{0,8},{8,0},{16,24},{24,16},{32,40},{40,32},{48,56},{56,48},{64,72... | collective-permute-start | bytes 73736 | tf_op jit(solution)/shard_map/ppermute | solution.py:42
  54.0 3.6 %collective-permute-start.10 = (bf16[96,128]{1,0:T(8,128)(2,1)S(1)}, bf16[96,128]{1,0:T(8,128)(2,1)S(1)}, u32[]{:S(2)}, u32[]{:S(2)}) collective-permute-start(bf16[96,128]{1,0:T(8,128)(2,1)S(1)} %get-tuple-element.50), channel_id=1, source_target_pairs={{1,2},{2,1},{3,4},{4,3},{5,6},{6,5},{9,10},{10,9},{11,12},{12,11},... | collective-permute-start | bytes 73736 | tf_op jit(solution)/shard_map/ppermute | solution.py:42
  57.6 1.9 %collective-permute-start.11 = (bf16[96,128]{1,0:T(8,128)(2,1)S(1)}, bf16[96,128]{1,0:T(8,128)(2,1)S(1)}, u32[]{:S(2)}, u32[]{:S(2)}) collective-permute-start(bf16[96,128]{1,0:T(8,128)(2,1)S(1)} %get-tuple-element.51), channel_id=1, source_target_pairs={{0,1},{1,0},{2,3},{3,2},{4,5},{5,4},{6,7},{7,6},{8,9},{9,8},{10,11... | collective-permute-start | bytes 73736 | tf_op jit(solution)/shard_map/ppermute | solution.py:42
  59.5 0.8 %copy.11 = bf16[1,1,3,625,128]{4,3,2,1,0:T(8,128)(2,1)} copy(bf16[1,1,3,625,128]{4,3,2,1,0:T(8,128)(2,1)S(1)} %get-tuple-element.52) | data formatting | bytes 960000
  60.3 0.0 collective-permute-done.8.a0
  60.3 0.0 collective-permute-done.9.a1
  60.3 0.4 collective-permute-done.11.a3
  60.7 0.6 %shard_map.109 = f32[1,1,3,32,128]{4,3,2,1,0:T(8,128)} custom-call(f32[96,128]{1,0:T(8,128)S(1)} %get-tuple-element.47.own_ref, bf16[96,128]{1,0:T(8,128)(2,1)S(1)} %collective-permute-done.8.a0, bf16[96,128]{1,0:T(8,128)(2,1)S(1)} %collective-permute-done.9.a1, bf16[96,128]{1,0:T(8,128)(2,1)S(1)} %collective-permute-done.10.a2, ...), custom_call_target="tpu_custom_call" | custom-call | tf_op jit(solution)/shard_map/pallas_call | solution.py:311
  (7 shorter events, 0.0 us)
Async XLA Ops:
  0.6 29.0 %copy-start.2 = (s32[1,1,3]{2,1,0:T(1,128)S(1)}, s32[1,1,3]{2,1,0:T(1,128)}, u32[]{:S(2)}) copy-start(s32[1,1,3]{2,1,0:T(1,128)} %order_ref.5) | copy-start | bytes 40
  0.6 29.0 %copy-start.1 = (s32[1,1,3,6]{3,1,2,0:T(1,128)S(1)}, s32[1,1,3,6]{3,1,2,0:T(1,128)}, u32[]{:S(2)}) copy-start(s32[1,1,3,6]{3,1,2,0:T(1,128)} %param.16) | copy-start | bytes 220
  4.8 24.8 %collective-permute-start = (bf16[3,128,128]{2,1,0:T(8,128)(2,1)S(1)}, bf16[3,128,128]{2,1,0:T(8,128)(2,1)S(1)}, u32[]{:S(2)}, u32[]{:S(2)}) collective-permute-start(bf16[3,128,128]{2,1,0:T(8,128)(2,1)S(1)} %get-tuple-element.31), channel_id=1, source_target_pairs={{8,16},{16,8},{24,32},{32,24},{40,48},{48,40},{56,64},{64,56},{72,... | collective-permute-start | bytes 294920 | tf_op jit(solution)/shard_map/ppermute | solution.py:42
  18.9 10.7 %collective-permute-start.1 = (bf16[3,128,128]{2,1,0:T(8,128)(2,1)S(1)}, bf16[3,128,128]{2,1,0:T(8,128)(2,1)S(1)}, u32[]{:S(2)}, u32[]{:S(2)}) collective-permute-start(bf16[3,128,128]{2,1,0:T(8,128)(2,1)S(1)} %get-tuple-element.32), channel_id=1, source_target_pairs={{0,8},{8,0},{16,24},{24,16},{32,40},{40,32},{48,56},{56,48},{64,72... | collective-permute-start | bytes 294920 | tf_op jit(solution)/shard_map/ppermute | solution.py:42
  20.8 8.7 %collective-permute-start.2 = (bf16[3,128,128]{2,1,0:T(8,128)(2,1)S(1)}, bf16[3,128,128]{2,1,0:T(8,128)(2,1)S(1)}, u32[]{:S(2)}, u32[]{:S(2)}) collective-permute-start(bf16[3,128,128]{2,1,0:T(8,128)(2,1)S(1)} %get-tuple-element.33), channel_id=1, source_target_pairs={{1,2},{2,1},{3,4},{4,3},{5,6},{6,5},{9,10},{10,9},{11,12},{12,11},... | collective-permute-start | bytes 294920 | tf_op jit(solution)/shard_map/ppermute | solution.py:42
  24.9 4.7 %collective-permute-start.3 = (bf16[3,128,128]{2,1,0:T(8,128)(2,1)S(1)}, bf16[3,128,128]{2,1,0:T(8,128)(2,1)S(1)}, u32[]{:S(2)}, u32[]{:S(2)}) collective-permute-start(bf16[3,128,128]{2,1,0:T(8,128)(2,1)S(1)} %get-tuple-element.34), channel_id=1, source_target_pairs={{0,1},{1,0},{2,3},{3,2},{4,5},{5,4},{6,7},{7,6},{8,9},{9,8},{10,11... | collective-permute-start | bytes 294920 | tf_op jit(solution)/shard_map/ppermute | solution.py:42
  31.9 12.9 %copy-start = (bf16[1,1,3,81,625]{4,3,2,1,0:T(8,128)(2,1)S(1)}, bf16[1,1,3,81,625]{4,3,2,1,0:T(8,128)(2,1)}, u32[]{:S(2)}) copy-start(bf16[1,1,3,81,625]{4,3,2,1,0:T(8,128)(2,1)} %shape_ref.1) | copy-start | bytes 911254
  31.9 12.9 %copy-start.3 = (s32[1,1,3,27]{3,1,2,0:T(1,128)S(1)}, s32[1,1,3,27]{3,1,2,0:T(1,128)}, u32[]{:S(2)}) copy-start(s32[1,1,3,27]{3,1,2,0:T(1,128)} %param.17) | copy-start | bytes 976
  31.9 12.8 %collective-permute-start.4 = (bf16[3,128,128]{2,1,0:T(8,128)(2,1)S(1)}, bf16[3,128,128]{2,1,0:T(8,128)(2,1)S(1)}, u32[]{:S(2)}, u32[]{:S(2)}) collective-permute-start(bf16[3,128,128]{2,1,0:T(8,128)(2,1)S(1)} %get-tuple-element.42), channel_id=1, source_target_pairs={{8,16},{16,8},{24,32},{32,24},{40,48},{48,40},{56,64},{64,56},{72,... | collective-permute-start | bytes 294920 | tf_op jit(solution)/shard_map/ppermute | solution.py:42
  35.0 9.7 %collective-permute-start.5 = (bf16[3,128,128]{2,1,0:T(8,128)(2,1)S(1)}, bf16[3,128,128]{2,1,0:T(8,128)(2,1)S(1)}, u32[]{:S(2)}, u32[]{:S(2)}) collective-permute-start(bf16[3,128,128]{2,1,0:T(8,128)(2,1)S(1)} %get-tuple-element.43), channel_id=1, source_target_pairs={{0,8},{8,0},{16,24},{24,16},{32,40},{40,32},{48,56},{56,48},{64,72... | collective-permute-start | bytes 294920 | tf_op jit(solution)/shard_map/ppermute | solution.py:42
  37.6 7.1 %collective-permute-start.6 = (bf16[3,128,128]{2,1,0:T(8,128)(2,1)S(1)}, bf16[3,128,128]{2,1,0:T(8,128)(2,1)S(1)}, u32[]{:S(2)}, u32[]{:S(2)}) collective-permute-start(bf16[3,128,128]{2,1,0:T(8,128)(2,1)S(1)} %get-tuple-element.44), channel_id=1, source_target_pairs={{1,2},{2,1},{3,4},{4,3},{5,6},{6,5},{9,10},{10,9},{11,12},{12,11},... | collective-permute-start | bytes 294920 | tf_op jit(solution)/shard_map/ppermute | solution.py:42
  41.5 3.3 %collective-permute-start.7 = (bf16[3,128,128]{2,1,0:T(8,128)(2,1)S(1)}, bf16[3,128,128]{2,1,0:T(8,128)(2,1)S(1)}, u32[]{:S(2)}, u32[]{:S(2)}) collective-permute-start(bf16[3,128,128]{2,1,0:T(8,128)(2,1)S(1)} %get-tuple-element.45), channel_id=1, source_target_pairs={{0,1},{1,0},{2,3},{3,2},{4,5},{5,4},{6,7},{7,6},{8,9},{9,8},{10,11... | collective-permute-start | bytes 294920 | tf_op jit(solution)/shard_map/ppermute | solution.py:42
  47.1 13.2 %collective-permute-start.8 = (bf16[96,128]{1,0:T(8,128)(2,1)S(1)}, bf16[96,128]{1,0:T(8,128)(2,1)S(1)}, u32[]{:S(2)}, u32[]{:S(2)}) collective-permute-start(bf16[96,128]{1,0:T(8,128)(2,1)S(1)} %get-tuple-element.48), channel_id=1, source_target_pairs={{8,16},{16,8},{24,32},{32,24},{40,48},{48,40},{56,64},{64,56},{72,... | collective-permute-start | bytes 73736 | tf_op jit(solution)/shard_map/ppermute | solution.py:42
  52.1 8.2 %collective-permute-start.9 = (bf16[96,128]{1,0:T(8,128)(2,1)S(1)}, bf16[96,128]{1,0:T(8,128)(2,1)S(1)}, u32[]{:S(2)}, u32[]{:S(2)}) collective-permute-start(bf16[96,128]{1,0:T(8,128)(2,1)S(1)} %get-tuple-element.49), channel_id=1, source_target_pairs={{0,8},{8,0},{16,24},{24,16},{32,40},{40,32},{48,56},{56,48},{64,72... | collective-permute-start | bytes 73736 | tf_op jit(solution)/shard_map/ppermute | solution.py:42
  54.0 6.3 %collective-permute-start.10 = (bf16[96,128]{1,0:T(8,128)(2,1)S(1)}, bf16[96,128]{1,0:T(8,128)(2,1)S(1)}, u32[]{:S(2)}, u32[]{:S(2)}) collective-permute-start(bf16[96,128]{1,0:T(8,128)(2,1)S(1)} %get-tuple-element.50), channel_id=1, source_target_pairs={{1,2},{2,1},{3,4},{4,3},{5,6},{6,5},{9,10},{10,9},{11,12},{12,11},... | collective-permute-start | bytes 73736 | tf_op jit(solution)/shard_map/ppermute | solution.py:42
  57.6 3.1 %collective-permute-start.11 = (bf16[96,128]{1,0:T(8,128)(2,1)S(1)}, bf16[96,128]{1,0:T(8,128)(2,1)S(1)}, u32[]{:S(2)}, u32[]{:S(2)}) collective-permute-start(bf16[96,128]{1,0:T(8,128)(2,1)S(1)} %get-tuple-element.51), channel_id=1, source_target_pairs={{0,1},{1,0},{2,3},{3,2},{4,5},{5,4},{6,7},{7,6},{8,9},{9,8},{10,11... | collective-permute-start | bytes 73736 | tf_op jit(solution)/shard_map/ppermute | solution.py:42
where the time goes:
time: 61.7 us; the launch traced here: 61.3 us
  starting transfers between devices  45.9 us (74%)
  Pallas kernels  13.3 us (22%)
  between operations  0.89 us (1%)
  local copies, waits for them, and re-layouts  0.8 us (1%)
    ppermute x12, starting transfers between devices, exchange(): lax.ppermute(sends[i], axis, swap_pairs(slot, lax.axis_size(axis)))  45.9 us
    pallas_call x6, Pallas kernels, call(): pl.pallas_call(kernel, in_specs=[SMEM] * len(scalars) + [ANY] * len(store...  13.3 us
  transfers between devices with their start and end apart: 12, of which 1 were waited for; matrix products, arithmetic and copies ran while one was open for 1% of the time, Pallas kernels for 7%

commit v1 on v0

--- a/solution.py
+++ b/solution.py
@@ -95,7 +95,7 @@
             rows_ref[at : at + FROWS, :] = dot(spreads[e], levels).astype(BF16)
 
 
-def build_face_operator(op_ref, faces, flux_ref, rows_ref, line_ref):
+def flux_factors(faces, flux_ref, line_ref):
     count = len(faces)
     line_ref[...] = jnp.zeros(line_ref.shape, F32)
     for e in range(ELEMS):
@@ -117,12 +117,13 @@
     pair = jnp.concatenate([high.astype(F32), low.astype(F32)], axis=0)
     line = iota((2 * VARS, BLOCK), 0)
     picks = (variable_of(iota((2 * VARS, BLOCK), 1)) == variable_of(line)).astype(BF16)
-    factors = dot(pair.T.astype(BF16), picks)
-    nodes = node_spread((NODES, BLOCK), 0)
-    wide = dot(rows_ref[...], nodes)
-    op = (wide * factors).astype(BF16)
-    for e in range(ELEMS):
-        op_ref[e] = op[e * count * FROWS : (e + 1) * count * FROWS]
+    return pair.T.astype(BF16), picks
+
+
+def build_face_operator(op_ref, e, count, factors, rows_ref):
+    at = slice(e * count * FROWS, (e + 1) * count * FROWS)
+    wide = dot(rows_ref[at, :], node_spread((NODES, BLOCK), 0))
+    op_ref[e] = (wide * dot(factors[0][at], factors[1])).astype(BF16)
 
 
 def build_trace_points(points_ref, order_ref, faces, trace_ref):
@@ -160,13 +161,12 @@
     sources = (order_hbm, trace_hbm, flux_hbm, adjoint_hbm)
     copies = start_copies(zip(sources, (order_ref, trace_ref, flux_ref, adjoint_ref)), sems)
     faces = slot_faces()
-    copies[0].wait()
-    copies[1].wait()
+    for copy in copies:
+        copy.wait()
     build_trace_rows(rows_ref, order_ref, faces, trace_ref)
-    copies[2].wait()
-    build_face_operator(op_ref, faces, flux_ref, rows_ref, line_ref)
-    copies[3].wait()
-    for e in range(ELEMS):
+    factors = flux_factors(faces, flux_ref, line_ref)
+    for e in range(ELEMS):
+        build_face_operator(op_ref, e, 4, factors, rows_ref)
         live = live_mask(order_ref[0, 0, e], (BLOCK, RHS))
         adjoint = jnp.where(live, adjoint_ref[0, 0, e], jnp.zeros((), BF16))
         tiles = dot(op_ref[e], adjoint).astype(BF16)
@@ -194,9 +194,12 @@
     rows_ref, line_ref, tile_ref, wide_ref, sum_ref, order_ref, near_ref, sems = refs[6:]
     sources = (order_hbm, near_hbm, rhs_hbm, inverse_hbm)
     copies = start_copies(zip(sources, (order_ref, near_ref, rhs_ref, inverse_ref)), sems)
-    copies[0].wait()
+    factors = flux_factors([4, 5], flux_ref, line_ref)
+    for copy in copies[:3]:
+        copy.wait()
     build_trace_rows(rows_ref, order_ref, [4, 5], trace_ref)
-    build_face_operator(local_op_ref, [4, 5], flux_ref, rows_ref, line_ref)
+    for e in range(ELEMS):
+        build_face_operator(local_op_ref, e, 2, factors, rows_ref)
     build_trace_points(local_points_ref, order_ref, [4, 5], trace_ref)
     build_trace_points(points_ref, order_ref, slot_faces(), trace_ref)
 
@@ -204,8 +207,6 @@
         live = live_mask(order_ref[0, 0, e], (BLOCK, RHS))
         return jnp.where(live, adjoint_ref[0, 0, e], jnp.zeros((), BF16))
 
-    copies[1].wait()
-    copies[2].wait()
     local_driven(
         near_ref, adjoints, rhs_ref, local_op_ref, local_points_ref,
         tile_ref, wide_ref, sum_ref, base_ref,

time: 61.7 us -> 61.2 us (level)
  no operation moved by 1% of the time
where the time goes in v1:
time: 61.2 us; the launch traced here: 60.8 us
  starting transfers between devices  45.9 us (75%)
  Pallas kernels  12.8 us (21%)
  between operations  0.89 us (1%)
  local copies, waits for them, and re-layouts  0.8 us (1%)
    ppermute x12, starting transfers between devices, exchange(): lax.ppermute(sends[i], axis, swap_pairs(slot, lax.axis_size(axis)))  45.9 us
    pallas_call x6, Pallas kernels, call(): pl.pallas_call(kernel, in_specs=[SMEM] * len(scalars) + [ANY] * len(store...  12.8 us
  transfers between devices with their start and end apart: 12, of which 1 were waited for; matrix products, arithmetic and copies ran while one was open for 1% of the time, Pallas kernels for 7%

profile of v1, /device:TPU:1, one launch (start us, length us, event | category | flops | bytes accessed | tf_op | source)
XLA Modules:
  0.0 60.8 jit_solution(445124209788452447)
XLA Ops:
  0.6 0.0 copy-start.2
  0.6 0.0 copy-start.1
  0.7 3.5 %shard_map.104 = (bf16[3,128,128]{2,1,0:T(8,128)(2,1)S(1)}, bf16[3,128,128]{2,1,0:T(8,128)(2,1)S(1)}, bf16[3,128,128]{2,1,0:T(8,128)(2,1)S(1)}, bf16[3,128,128]{...) custom-call(s32[1,1,3]{2,1,0:T(1,128)} %order_ref.5, ...), custom_call_target="tpu_custom_call" | custom-call | tf_op jit(solution)/shard_map/pallas_call | solution.py:312
  4.2 14.1 %collective-permute-start = (bf16[3,128,128]{2,1,0:T(8,128)(2,1)S(1)}, bf16[3,128,128]{2,1,0:T(8,128)(2,1)S(1)}, u32[]{:S(2)}, u32[]{:S(2)}) collective-permute-start(bf16[3,128,128]{2,1,0:T(8,128)(2,1)S(1)} %get-tuple-element.31), channel_id=1, source_target_pairs={{8,16},{16,8},{24,32},{32,24},{40,48},{48,40},{56,64},{64,56},{72,... | collective-permute-start | bytes 294920 | tf_op jit(solution)/shard_map/ppermute | solution.py:42
  18.3 1.9 %collective-permute-start.1 = (bf16[3,128,128]{2,1,0:T(8,128)(2,1)S(1)}, bf16[3,128,128]{2,1,0:T(8,128)(2,1)S(1)}, u32[]{:S(2)}, u32[]{:S(2)}) collective-permute-start(bf16[3,128,128]{2,1,0:T(8,128)(2,1)S(1)} %get-tuple-element.32), channel_id=1, source_target_pairs={{0,8},{8,0},{16,24},{24,16},{32,40},{40,32},{48,56},{56,48},{64,72... | collective-permute-start | bytes 294920 | tf_op jit(solution)/shard_map/ppermute | solution.py:42
  20.3 4.0 %collective-permute-start.2 = (bf16[3,128,128]{2,1,0:T(8,128)(2,1)S(1)}, bf16[3,128,128]{2,1,0:T(8,128)(2,1)S(1)}, u32[]{:S(2)}, u32[]{:S(2)}) collective-permute-start(bf16[3,128,128]{2,1,0:T(8,128)(2,1)S(1)} %get-tuple-element.33), channel_id=1, source_target_pairs={{1,2},{2,1},{3,4},{4,3},{5,6},{6,5},{9,10},{10,9},{11,12},{12,11},... | collective-permute-start | bytes 294920 | tf_op jit(solution)/shard_map/ppermute | solution.py:42
  24.3 1.9 %collective-permute-start.3 = (bf16[3,128,128]{2,1,0:T(8,128)(2,1)S(1)}, bf16[3,128,128]{2,1,0:T(8,128)(2,1)S(1)}, u32[]{:S(2)}, u32[]{:S(2)}) collective-permute-start(bf16[3,128,128]{2,1,0:T(8,128)(2,1)S(1)} %get-tuple-element.34), channel_id=1, source_target_pairs={{0,1},{1,0},{2,3},{3,2},{4,5},{5,4},{6,7},{7,6},{8,9},{9,8},{10,11... | collective-permute-start | bytes 294920 | tf_op jit(solution)/shard_map/ppermute | solution.py:42
  26.2 2.8 %shard_map.105 = (f32[3,625,128]{2,1,0:T(8,128)S(1)}, bf16[3,128,125]{2,1,0:T(8,128)(2,1)S(1)}, bf16[3,256,625]{2,1,0:T(8,128)(2,1)S(1)}, bf16[3,64,125]{2,1,0:T...) custom-call(s32[1,1,3]{2,1,0:T(1,128)} %order_ref.5, ...), custom_call_target="tpu_custom_call" | custom-call | tf_op jit(solution)/shard_map/pallas_call | solution.py:312
  29.0 0.0 collective-permute-done.a0
  29.0 0.0 collective-permute-done.1.a1
  29.0 0.0 collective-permute-done.2.a2
  29.0 0.0 collective-permute-done.3.a3
  29.1 2.3 %shard_map.106 = (bf16[3,128,128]{2,1,0:T(8,128)(2,1)S(1)}, bf16[3,128,128]{2,1,0:T(8,128)(2,1)S(1)}, bf16[3,128,128]{2,1,0:T(8,128)(2,1)S(1)}, bf16[3,128,128]{2,1,0:T(8,128)(2,1)S(1)}, bf16[3,625,128]{2,1,0:T(8,128)(2,1)S(1)}) custom-call(s32[1,1,3]{2,1,0:T(1,128)S(1)} %copy-done.2, s32[3,1,6]{2,1,0:T(1,128)S(1)} %bitcast.6, ...), custom_call_target="tpu_custom_call" | custom-call | tf_op jit(solution)/shard_map/pallas_call | solution.py:312
  31.3 0.0 copy-start
  31.3 0.0 copy-start.3
  31.4 3.1 %collective-permute-start.4 = (bf16[3,128,128]{2,1,0:T(8,128)(2,1)S(1)}, bf16[3,128,128]{2,1,0:T(8,128)(2,1)S(1)}, u32[]{:S(2)}, u32[]{:S(2)}) collective-permute-start(bf16[3,128,128]{2,1,0:T(8,128)(2,1)S(1)} %get-tuple-element.42), channel_id=1, source_target_pairs={{8,16},{16,8},{24,32},{32,24},{40,48},{48,40},{56,64},{64,56},{72,... | collective-permute-start | bytes 294920 | tf_op jit(solution)/shard_map/ppermute | solution.py:42
  34.5 2.6 %collective-permute-start.5 = (bf16[3,128,128]{2,1,0:T(8,128)(2,1)S(1)}, bf16[3,128,128]{2,1,0:T(8,128)(2,1)S(1)}, u32[]{:S(2)}, u32[]{:S(2)}) collective-permute-start(bf16[3,128,128]{2,1,0:T(8,128)(2,1)S(1)} %get-tuple-element.43), channel_id=1, source_target_pairs={{0,8},{8,0},{16,24},{24,16},{32,40},{40,32},{48,56},{56,48},{64,72... | collective-permute-start | bytes 294920 | tf_op jit(solution)/shard_map/ppermute | solution.py:42
  37.1 3.9 %collective-permute-start.6 = (bf16[3,128,128]{2,1,0:T(8,128)(2,1)S(1)}, bf16[3,128,128]{2,1,0:T(8,128)(2,1)S(1)}, u32[]{:S(2)}, u32[]{:S(2)}) collective-permute-start(bf16[3,128,128]{2,1,0:T(8,128)(2,1)S(1)} %get-tuple-element.44), channel_id=1, source_target_pairs={{1,2},{2,1},{3,4},{4,3},{5,6},{6,5},{9,10},{10,9},{11,12},{12,11},... | collective-permute-start | bytes 294920 | tf_op jit(solution)/shard_map/ppermute | solution.py:42
  40.9 1.9 %collective-permute-start.7 = (bf16[3,128,128]{2,1,0:T(8,128)(2,1)S(1)}, bf16[3,128,128]{2,1,0:T(8,128)(2,1)S(1)}, u32[]{:S(2)}, u32[]{:S(2)}) collective-permute-start(bf16[3,128,128]{2,1,0:T(8,128)(2,1)S(1)} %get-tuple-element.45), channel_id=1, source_target_pairs={{0,1},{1,0},{2,3},{3,2},{4,5},{5,4},{6,7},{7,6},{8,9},{9,8},{10,11... | collective-permute-start | bytes 294920 | tf_op jit(solution)/shard_map/ppermute | solution.py:42
  42.9 1.3 %shard_map.107.base_ref = f32[3,625,128]{2,1,0:T(8,128)S(1)} custom-call(s32[1,1,3]{2,1,0:T(1,128)S(1)} %copy-done.2, s32[3,1,6]{2,1,0:T(1,128)S(1)} %bitcast.7, bf16[3,625,128]{2,1,0:T(8,128)(2,1)S(1)} %get-tuple-element.38.adjoint_ref, bf16[1,1,3,625,128]{4,3,2,1,0:T(8,128)(2,1)S(1)} %get-tuple-element.39.rhs_ref, ...), custom_call_target="tpu_custom_call" | custom-call | tf_op jit(solution)/shard_map/pallas_call | solution.py:312
  44.2 0.0 collective-permute-done.4.a0
  44.2 0.0 collective-permute-done.5.a1
  44.2 0.0 collective-permute-done.6.a2
  44.2 2.3 %shard_map.108 = (bf16[1,1,3,625,128]{4,3,2,1,0:T(8,128)(2,1)S(1)}, f32[96,128]{1,0:T(8,128)S(1)}, bf16[96,128]{1,0:T(8,128)(2,1)S(1)}, bf16[96,128]{1,0:T(8,128...) custom-call(s32[1,1,3]{2,1,0:T(1,128)S(1)} %copy-done.2, s32[3,1,6]{2,1,0:T(1,128)S(1)} %bitcast.8, ...), custom_call_target="tpu_custom_call" | custom-call | tf_op jit(solution)/shard_map/pallas_call | solution.py:312
  46.5 5.0 %collective-permute-start.8 = (bf16[96,128]{1,0:T(8,128)(2,1)S(1)}, bf16[96,128]{1,0:T(8,128)(2,1)S(1)}, u32[]{:S(2)}, u32[]{:S(2)}) collective-permute-start(bf16[96,128]{1,0:T(8,128)(2,1)S(1)} %get-tuple-element.48), channel_id=1, source_target_pairs={{8,16},{16,8},{24,32},{32,24},{40,48},{48,40},{56,64},{64,56},{72,... | collective-permute-start | bytes 73736 | tf_op jit(solution)/shard_map/ppermute | solution.py:42
  51.5 1.9 %collective-permute-start.9 = (bf16[96,128]{1,0:T(8,128)(2,1)S(1)}, bf16[96,128]{1,0:T(8,128)(2,1)S(1)}, u32[]{:S(2)}, u32[]{:S(2)}) collective-permute-start(bf16[96,128]{1,0:T(8,128)(2,1)S(1)} %get-tuple-element.49), channel_id=1, source_target_pairs={{0,8},{8,0},{16,24},{24,16},{32,40},{40,32},{48,56},{56,48},{64,72... | collective-permute-start | bytes 73736 | tf_op jit(solution)/shard_map/ppermute | solution.py:42
  53.5 3.6 %collective-permute-start.10 = (bf16[96,128]{1,0:T(8,128)(2,1)S(1)}, bf16[96,128]{1,0:T(8,128)(2,1)S(1)}, u32[]{:S(2)}, u32[]{:S(2)}) collective-permute-start(bf16[96,128]{1,0:T(8,128)(2,1)S(1)} %get-tuple-element.50), channel_id=1, source_target_pairs={{1,2},{2,1},{3,4},{4,3},{5,6},{6,5},{9,10},{10,9},{11,12},{12,11},... | collective-permute-start | bytes 73736 | tf_op jit(solution)/shard_map/ppermute | solution.py:42
  57.0 1.9 %collective-permute-start.11 = (bf16[96,128]{1,0:T(8,128)(2,1)S(1)}, bf16[96,128]{1,0:T(8,128)(2,1)S(1)}, u32[]{:S(2)}, u32[]{:S(2)}) collective-permute-start(bf16[96,128]{1,0:T(8,128)(2,1)S(1)} %get-tuple-element.51), channel_id=1, source_target_pairs={{0,1},{1,0},{2,3},{3,2},{4,5},{5,4},{6,7},{7,6},{8,9},{9,8},{10,11... | collective-permute-start | bytes 73736 | tf_op jit(solution)/shard_map/ppermute | solution.py:42
  59.0 0.8 %copy.11 = bf16[1,1,3,625,128]{4,3,2,1,0:T(8,128)(2,1)} copy(bf16[1,1,3,625,128]{4,3,2,1,0:T(8,128)(2,1)S(1)} %get-tuple-element.52) | data formatting | bytes 960000
  59.7 0.0 collective-permute-done.10.a2
  59.8 0.4 collective-permute-done.11.a3
  60.1 0.6 %shard_map.109 = f32[1,1,3,32,128]{4,3,2,1,0:T(8,128)} custom-call(f32[96,128]{1,0:T(8,128)S(1)} %get-tuple-element.47.own_ref, bf16[96,128]{1,0:T(8,128)(2,1)S(1)} %collective-permute-done.8.a0, bf16[96,128]{1,0:T(8,128)(2,1)S(1)} %collective-permute-done.9.a1, bf16[96,128]{1,0:T(8,128)(2,1)S(1)} %collective-permute-done.10.a2, ...), custom_call_target="tpu_custom_call" | custom-call | tf_op jit(solution)/shard_map/pallas_call | solution.py:312
  (7 shorter events, 0.0 us)
Async XLA Ops:
  0.6 28.4 %copy-start.2 = (s32[1,1,3]{2,1,0:T(1,128)S(1)}, s32[1,1,3]{2,1,0:T(1,128)}, u32[]{:S(2)}) copy-start(s32[1,1,3]{2,1,0:T(1,128)} %order_ref.5) | copy-start | bytes 40
  0.6 28.4 %copy-start.1 = (s32[1,1,3,6]{3,1,2,0:T(1,128)S(1)}, s32[1,1,3,6]{3,1,2,0:T(1,128)}, u32[]{:S(2)}) copy-start(s32[1,1,3,6]{3,1,2,0:T(1,128)} %param.16) | copy-start | bytes 220
  4.2 24.8 %collective-permute-start = (bf16[3,128,128]{2,1,0:T(8,128)(2,1)S(1)}, bf16[3,128,128]{2,1,0:T(8,128)(2,1)S(1)}, u32[]{:S(2)}, u32[]{:S(2)}) collective-permute-start(bf16[3,128,128]{2,1,0:T(8,128)(2,1)S(1)} %get-tuple-element.31), channel_id=1, source_target_pairs={{8,16},{16,8},{24,32},{32,24},{40,48},{48,40},{56,64},{64,56},{72,... | collective-permute-start | bytes 294920 | tf_op jit(solution)/shard_map/ppermute | solution.py:42
  18.3 10.7 %collective-permute-start.1 = (bf16[3,128,128]{2,1,0:T(8,128)(2,1)S(1)}, bf16[3,128,128]{2,1,0:T(8,128)(2,1)S(1)}, u32[]{:S(2)}, u32[]{:S(2)}) collective-permute-start(bf16[3,128,128]{2,1,0:T(8,128)(2,1)S(1)} %get-tuple-element.32), channel_id=1, source_target_pairs={{0,8},{8,0},{16,24},{24,16},{32,40},{40,32},{48,56},{56,48},{64,72... | collective-permute-start | bytes 294920 | tf_op jit(solution)/shard_map/ppermute | solution.py:42
  20.3 8.8 %collective-permute-start.2 = (bf16[3,128,128]{2,1,0:T(8,128)(2,1)S(1)}, bf16[3,128,128]{2,1,0:T(8,128)(2,1)S(1)}, u32[]{:S(2)}, u32[]{:S(2)}) collective-permute-start(bf16[3,128,128]{2,1,0:T(8,128)(2,1)S(1)} %get-tuple-element.33), channel_id=1, source_target_pairs={{1,2},{2,1},{3,4},{4,3},{5,6},{6,5},{9,10},{10,9},{11,12},{12,11},... | collective-permute-start | bytes 294920 | tf_op jit(solution)/shard_map/ppermute | solution.py:42
  24.3 4.7 %collective-permute-start.3 = (bf16[3,128,128]{2,1,0:T(8,128)(2,1)S(1)}, bf16[3,128,128]{2,1,0:T(8,128)(2,1)S(1)}, u32[]{:S(2)}, u32[]{:S(2)}) collective-permute-start(bf16[3,128,128]{2,1,0:T(8,128)(2,1)S(1)} %get-tuple-element.34), channel_id=1, source_target_pairs={{0,1},{1,0},{2,3},{3,2},{4,5},{5,4},{6,7},{7,6},{8,9},{9,8},{10,11... | collective-permute-start | bytes 294920 | tf_op jit(solution)/shard_map/ppermute | solution.py:42
  31.3 12.9 %copy-start = (bf16[1,1,3,81,625]{4,3,2,1,0:T(8,128)(2,1)S(1)}, bf16[1,1,3,81,625]{4,3,2,1,0:T(8,128)(2,1)}, u32[]{:S(2)}) copy-start(bf16[1,1,3,81,625]{4,3,2,1,0:T(8,128)(2,1)} %shape_ref.1) | copy-start | bytes 911254
  31.3 12.9 %copy-start.3 = (s32[1,1,3,27]{3,1,2,0:T(1,128)S(1)}, s32[1,1,3,27]{3,1,2,0:T(1,128)}, u32[]{:S(2)}) copy-start(s32[1,1,3,27]{3,1,2,0:T(1,128)} %param.17) | copy-start | bytes 976
  31.4 12.8 %collective-permute-start.4 = (bf16[3,128,128]{2,1,0:T(8,128)(2,1)S(1)}, bf16[3,128,128]{2,1,0:T(8,128)(2,1)S(1)}, u32[]{:S(2)}, u32[]{:S(2)}) collective-permute-start(bf16[3,128,128]{2,1,0:T(8,128)(2,1)S(1)} %get-tuple-element.42), channel_id=1, source_target_pairs={{8,16},{16,8},{24,32},{32,24},{40,48},{48,40},{56,64},{64,56},{72,... | collective-permute-start | bytes 294920 | tf_op jit(solution)/shard_map/ppermute | solution.py:42
  34.5 9.7 %collective-permute-start.5 = (bf16[3,128,128]{2,1,0:T(8,128)(2,1)S(1)}, bf16[3,128,128]{2,1,0:T(8,128)(2,1)S(1)}, u32[]{:S(2)}, u32[]{:S(2)}) collective-permute-start(bf16[3,128,128]{2,1,0:T(8,128)(2,1)S(1)} %get-tuple-element.43), channel_id=1, source_target_pairs={{0,8},{8,0},{16,24},{24,16},{32,40},{40,32},{48,56},{56,48},{64,72... | collective-permute-start | bytes 294920 | tf_op jit(solution)/shard_map/ppermute | solution.py:42
  37.1 7.1 %collective-permute-start.6 = (bf16[3,128,128]{2,1,0:T(8,128)(2,1)S(1)}, bf16[3,128,128]{2,1,0:T(8,128)(2,1)S(1)}, u32[]{:S(2)}, u32[]{:S(2)}) collective-permute-start(bf16[3,128,128]{2,1,0:T(8,128)(2,1)S(1)} %get-tuple-element.44), channel_id=1, source_target_pairs={{1,2},{2,1},{3,4},{4,3},{5,6},{6,5},{9,10},{10,9},{11,12},{12,11},... | collective-permute-start | bytes 294920 | tf_op jit(solution)/shard_map/ppermute | solution.py:42
  40.9 3.3 %collective-permute-start.7 = (bf16[3,128,128]{2,1,0:T(8,128)(2,1)S(1)}, bf16[3,128,128]{2,1,0:T(8,128)(2,1)S(1)}, u32[]{:S(2)}, u32[]{:S(2)}) collective-permute-start(bf16[3,128,128]{2,1,0:T(8,128)(2,1)S(1)} %get-tuple-element.45), channel_id=1, source_target_pairs={{0,1},{1,0},{2,3},{3,2},{4,5},{5,4},{6,7},{7,6},{8,9},{9,8},{10,11... | collective-permute-start | bytes 294920 | tf_op jit(solution)/shard_map/ppermute | solution.py:42
  46.5 13.2 %collective-permute-start.8 = (bf16[96,128]{1,0:T(8,128)(2,1)S(1)}, bf16[96,128]{1,0:T(8,128)(2,1)S(1)}, u32[]{:S(2)}, u32[]{:S(2)}) collective-permute-start(bf16[96,128]{1,0:T(8,128)(2,1)S(1)} %get-tuple-element.48), channel_id=1, source_target_pairs={{8,16},{16,8},{24,32},{32,24},{40,48},{48,40},{56,64},{64,56},{72,... | collective-permute-start | bytes 73736 | tf_op jit(solution)/shard_map/ppermute | solution.py:42
  51.5 8.2 %collective-permute-start.9 = (bf16[96,128]{1,0:T(8,128)(2,1)S(1)}, bf16[96,128]{1,0:T(8,128)(2,1)S(1)}, u32[]{:S(2)}, u32[]{:S(2)}) collective-permute-start(bf16[96,128]{1,0:T(8,128)(2,1)S(1)} %get-tuple-element.49), channel_id=1, source_target_pairs={{0,8},{8,0},{16,24},{24,16},{32,40},{40,32},{48,56},{56,48},{64,72... | collective-permute-start | bytes 73736 | tf_op jit(solution)/shard_map/ppermute | solution.py:42
  53.5 6.3 %collective-permute-start.10 = (bf16[96,128]{1,0:T(8,128)(2,1)S(1)}, bf16[96,128]{1,0:T(8,128)(2,1)S(1)}, u32[]{:S(2)}, u32[]{:S(2)}) collective-permute-start(bf16[96,128]{1,0:T(8,128)(2,1)S(1)} %get-tuple-element.50), channel_id=1, source_target_pairs={{1,2},{2,1},{3,4},{4,3},{5,6},{6,5},{9,10},{10,9},{11,12},{12,11},... | collective-permute-start | bytes 73736 | tf_op jit(solution)/shard_map/ppermute | solution.py:42
  57.0 3.1 %collective-permute-start.11 = (bf16[96,128]{1,0:T(8,128)(2,1)S(1)}, bf16[96,128]{1,0:T(8,128)(2,1)S(1)}, u32[]{:S(2)}, u32[]{:S(2)}) collective-permute-start(bf16[96,128]{1,0:T(8,128)(2,1)S(1)} %get-tuple-element.51), channel_id=1, source_target_pairs={{0,1},{1,0},{2,3},{3,2},{4,5},{5,4},{6,7},{7,6},{8,9},{9,8},{10,11... | collective-permute-start | bytes 73736 | tf_op jit(solution)/shard_map/ppermute | solution.py:42
